TPU v7x, 512 devices: a whole 4x8x8 slice. The times are simulated.
512 devices in a mesh: expert: 8 (over z_hi, core), tensor: 16 (over y, z_lo), dp: 4 (over x).
Axes of the slice: x: 4, y: 8, z: 8 (z_hi: 4, z_lo: 2; z = z_hi * 2 + z_lo), core: 2. Of those that a mesh axis runs over, the one named last changes fastest.
Arguments:
- tokens: bfloat16 [3072, 3072], P(('expert', 'dp'), 'tensor'), may hold values from -6 to 6
- out_grad: bfloat16 [3072, 3072], P(('expert', 'dp'), 'tensor'), may hold values from -6 to 6
- gates: float32 [3072, 2], P(('expert', 'dp')), may hold values from 0.2 to 1
- expert_ids: int32 [3072, 2], P(('expert', 'dp')), may hold values from 0 to 7, all different within a row; in each aligned block of 96 rows (0 to 95, 96 to 191, ...) at most 42 rows name the same one
- w_gate_up: bfloat16 [8, 2, 3072, 8192], P('expert', None, 'dp', 'tensor'), may hold values from -0.109375 to 0.109375
- w_down: bfloat16 [8, 8192, 3072], P('expert', 'tensor', 'dp'), may hold values from -0.109375 to 0.109375
Outputs:
- input_grad: bfloat16 [3072, 3072], P(('expert', 'dp'), 'tensor')
Inputs may be any that keep to these rules, and one draw needn't show every extreme that they name: `expert_ids`: the two experts of a row differ; among the rows of one device no expert is named more than 42 times.
All inputs are finite; a program needn't handle non-finite values.
Results may differ from a plain program's by a relative error of at most 0.019.
Values may be sent and summed in bfloat16 or wider, within the bound.
A program may use at most 64 MiB of HBM per device.

v0:
```python
import jax
import jax.numpy as jnp
from jax import lax
from jax.sharding import PartitionSpec as P


def body(tokens, out_grad, gates, expert_ids, w_gate_up, w_down):
    width = tokens.shape[1]
    count = tokens.shape[0]
    experts = lax.axis_size("expert")
    capacity = max(7 * count // 16, 2 * count // experts)
    slot_total = experts * capacity
    choose = (expert_ids[:, :, None] == jnp.arange(experts, dtype=jnp.int32)).astype(jnp.int32)
    per_token = jnp.sum(choose, axis=1)
    before = jnp.cumsum(per_token, axis=0) - per_token
    position = jnp.sum(choose * before[:, None, :], axis=2)
    target = expert_ids * capacity + position
    select = jnp.any(
        target[None, :, :] == jnp.arange(slot_total, dtype=jnp.int32)[:, None, None], axis=2
    ).astype(jnp.bfloat16)
    stacked = jnp.concatenate([tokens, out_grad], axis=1)
    contract = (((1,), (1,)), ((), ()))
    outgoing = jnp.dot(select, stacked, preferred_element_type=jnp.float32).astype(jnp.bfloat16)
    outgoing = outgoing.reshape(experts, capacity, 2 * width)
    arrived = lax.all_to_all(outgoing, "expert", split_axis=0, concat_axis=0, tiled=True).reshape(
        slot_total, 2 * width
    )
    full_gu, full_down = (
        lax.all_gather(w_gate_up, "dp", axis=2, tiled=True),
        lax.all_gather(w_down, "dp", axis=2, tiled=True),
    )
    gate_up = full_gu[0]
    down = full_down[0]
    piece = lax.all_gather(arrived, "tensor", axis=1, tiled=True)
    rows_here = piece.shape[0]
    shards = piece.shape[1] // (2 * width)
    parts = piece.reshape(rows_here, shards, 2, width)
    inputs = parts[:, :, 0, :].reshape(rows_here, shards * width)
    grads = parts[:, :, 1, :].reshape(rows_here, shards * width)
    gate_pre = jnp.dot(inputs, gate_up[0], preferred_element_type=jnp.float32)
    up_pre = jnp.dot(inputs, gate_up[1], preferred_element_type=jnp.float32)
    hidden_grad = lax.dot_general(grads, down, contract, preferred_element_type=jnp.float32)
    gate_pre, up_pre, hidden_grad = (gate_pre, up_pre, hidden_grad)
    sigma = jax.nn.sigmoid(gate_pre)
    up_grad = (hidden_grad * gate_pre * sigma).astype(jnp.bfloat16)
    gate_grad = (hidden_grad * up_pre * sigma * (1.0 + gate_pre * (1.0 - sigma))).astype(
        jnp.bfloat16
    )
    partial_rows = lax.dot_general(
        gate_grad, gate_up[0], contract, preferred_element_type=jnp.float32
    )
    partial_rows = partial_rows + lax.dot_general(
        up_grad, gate_up[1], contract, preferred_element_type=jnp.float32
    )
    summed = lax.psum_scatter(
        partial_rows.astype(jnp.bfloat16), "tensor", scatter_dimension=1, tiled=True
    )
    returned = summed.reshape(experts, capacity, width)
    back = lax.all_to_all(returned, "expert", split_axis=0, concat_axis=0, tiled=True).reshape(
        slot_total, width
    )
    picked = back[target].astype(jnp.float32)
    result = jnp.sum(gates[:, :, None] * picked, axis=1)
    return result.astype(jnp.bfloat16)


def solution(mesh):
    return jax.shard_map(
        body,
        mesh=mesh,
        in_specs=(
            P(("expert", "dp"), "tensor"),
            P(("expert", "dp"), "tensor"),
            P(("expert", "dp"), None),
            P(("expert", "dp"), None),
            P("expert", None, "dp", "tensor"),
            P("expert", "tensor", "dp"),
        ),
        out_specs=P(("expert", "dp"), "tensor"),
        check_vma=False,
    )
```

profile of v0, /device:TPU:7, one launch (start us, length us, event | category | flops | bytes accessed | tf_op | source)
XLA Modules:
  0.0 378.5 jit_solution(5035111132521601672)
XLA Ops:
  6.5 0.0 all-gather.4.cloned.1.call-start
  6.5 0.7 convert_reduce_fusion
  7.2 0.1 copy.18
  7.3 0.1 reduce_window_sum.11
  7.5 0.1 copy.20
  7.5 0.7 select_reduce_fusion
  8.2 0.7 compare_select_fusion
  8.9 0.1 fusion.14
  9.0 1.2 convolution_convert_fusion
  10.2 0.1 reshape.31
  10.3 23.5 %all_to_all.10 = bf16[8,42,384]{2,1,0:T(8,128)(2,1)S(1)} all-to-all(bf16[8,42,384]{2,1,0:T(8,128)(2,1)S(1)} %reshape.31), channel_id=1, replica_groups=mesh['expert'=8,'tensor'=16,'dp'=4] {'expert'}, dimensions={0} | all-to-all | bytes 516096 | tf_op jit(solution)/shard_map/all_to_all | solution.py:25
  33.8 0.8 reshape.32
  34.6 0.0 all-gather.4.cloned.1.call-update
  34.6 0.0 all-gather.6.cloned.1.call-start
  34.7 0.7 all-gather.6.cloned.1.call-update
  35.4 0.0 all-gather.8.cloned.1.call-start
  35.4 0.7 all-gather.8.cloned.1.call-update
  36.1 0.0 reduce-scatter.2.cloned.1.call-start
  36.2 93.5 %all-gather.4.cloned.1.call-done = bf16[336,6144]{1,0:T(8,128)(2,1)} async-done(((bf16[336,384]{1,0:T(8,128)(2,1)}), bf16[336,6144]{1,0:T(8,128)(2,1)}) %all-gather.4.cloned.1.call-update) | async-done | bytes 4128784 | tf_op jit(solution)/shard_map/all_gather | solution.py:34
  129.6 6.5 %copy.21 = bf16[336,6144]{0,1:T(8,128)(2,1)} copy(bf16[336,6144]{1,0:T(8,128)(2,1)} %all-gather.4.cloned.1.call-done) | data formatting | bytes 8257536 | tf_op jit(solution)/shard_map/all_gather | solution.py:34
  136.2 4.4 %fusion.21 = (bf16[336,16,1,192]{0,3,2,1:T(8,128)(2,1)S(1)}, bf16[336,16,1,192]{0,3,2,1:T(8,128)(2,1)}) fusion(bf16[336,16,2,192]{0,3,2,1:T(8,128)(2,1)} %bitcast.28), kind=kLoop, calls=%fused_computation.36 | loop fusion | bytes 8257536 | tf_op jit(solution)/shard_map/slice | solution.py:38
  140.5 36.9 %all-gather.6.cloned.1.call-done = bf16[1,512,3072]{2,1,0:T(8,128)(2,1)} async-done(((bf16[1,512,768]{2,1,0:T(8,128)(2,1)}), bf16[1,512,3072]{2,1,0:T(8,128)(2,1)}) %all-gather.6.cloned.1.call-update) | async-done | bytes 3145744 | tf_op jit(solution)/shard_map/all_gather | solution.py:30
  177.4 4.2 %fusion = f32[336,512]{1,0:T(8,128)S(1)} fusion(bf16[336,3072]{0,1:T(8,128)(2,1)} %bitcast.31, bf16[1,512,3072]{2,1,0:T(8,128)(2,1)} %all-gather.6.cloned.1.call-done), kind=kOutput, calls=%fused_computation.4 | convolution fusion | flops 1056964608 | bytes 5898240 | tf_op jit(solution)/shard_map/dot_general | solution.py:42
  181.7 69.1 %all-gather.8.cloned.1.call-done = bf16[1,2,3072,512]{3,2,1,0:T(8,128)(2,1)} async-done(((bf16[1,2,768,512]{3,2,1,0:T(8,128)(2,1)}), bf16[1,2,3072,512]{3,2,1,0:T(8,128)(2,1)}) %all-gather.8.cloned.1.call-update) | async-done | bytes 6291472 | tf_op jit(solution)/shard_map/all_gather | solution.py:29
  250.8 4.0 %fusion.4 = f32[336,512]{1,0:T(8,128)} fusion(bf16[336,3072]{0,1:T(8,128)(2,1)S(1)} %bitcast.29, bf16[1,2,3072,512]{3,2,1,0:T(8,128)(2,1)} %all-gather.8.cloned.1.call-done), kind=kOutput, calls=%fused_computation.8 | convolution fusion | flops 1056964608 | bytes 5898240 | tf_op jit(solution)/shard_map/dot_general | solution.py:40
  254.8 8.4 %fusion.3 = f32[336,3072]{0,1:T(8,128)} fusion(bf16[1,2,3072,512]{3,2,1,0:T(8,128)(2,1)} %all-gather.8.cloned.1.call-done, f32[336,512]{1,0:T(8,128)S(1)} %fusion, bf16[336,3072]{0,1:T(8,128)(2,1)S(1)} %bitcast.30, f32[336,512]{1,0:T(8,128)} %fusion.4), kind=kOutput, calls=%fused_computation.7 | convolution fusion | flops 2115649536 | bytes 13860864 | tf_op jit(solution)/shard_map/dot_general | solution.py:49
  263.2 6.8 %add_convert_fusion = bf16[336,3072]{0,1:T(8,128)(2,1)} fusion(f32[336,3072]{0,1:T(8,128)} %fusion.3, bf16[1,2,3072,512]{3,2,1,0:T(8,128)(2,1)} %all-gather.8.cloned.1.call-done, f32[336,512]{1,0:T(8,128)S(1)} %fusion, f32[336,512]{1,0:T(8,128)} %fusion.4), kind=kOutput, calls=%fused_computation.1 | convolution fusion | flops 1060061184 | bytes 11304960 | tf_op jit(solution)/shard_map/dot_general | solution.py:52
  270.0 0.0 copy-start
  270.0 0.0 reduce-scatter.2.cloned.1.call-update
  270.1 71.5 %reduce-scatter.2.cloned.1.call-done = bf16[336,192]{0,1:T(8,128)(2,1)} async-done(((bf16[336,3072]{0,1:T(8,128)(2,1)}), bf16[336,192]{0,1:T(8,128)(2,1)}) %reduce-scatter.2.cloned.1.call-update) | async-done | bytes 129040 | tf_op jit(solution)/shard_map/reduce_scatter | solution.py:55
  341.5 1.0 copy.22
  342.6 0.7 reshape.34
  343.3 17.9 %all-to-all-start.1 = ((bf16[8,42,192]{2,1,0:T(8,128)(2,1)}), bf16[8,42,192]{2,1,0:T(8,128)(2,1)S(1)}, u32[]{:S(2)}, u32[]{:S(2)}) async-start(bf16[8,42,192]{2,1,0:T(8,128)(2,1)} %reshape.34), calls=%async_computation.2 | async-start | bytes 393216 | tf_op jit(solution)/shard_map/all_to_all | solution.py:59
  361.2 0.1 copy.23
  361.3 0.1 reshape.38
  361.4 0.0 copy-done
  361.4 0.1 copy.17
  361.5 8.3 %all-to-all-done.1 = bf16[8,42,192]{2,1,0:T(8,128)(2,1)S(1)} async-done(((bf16[8,42,192]{2,1,0:T(8,128)(2,1)}), bf16[8,42,192]{2,1,0:T(8,128)(2,1)S(1)}, u32[]{:S(2)}, u32[]{:S(2)}) %all-to-all-start.1) | async-done | bytes 129056 | tf_op jit(solution)/shard_map/all_to_all | solution.py:59
  369.8 0.1 reshape.35
  369.9 1.0 gather_fusion
  370.9 0.1 reshape.46
  371.0 1.0 multiply_reduce_fusion
  (2 shorter events, 0.0 us)
Async XLA Ops:
  6.5 123.1 %all-gather.4.cloned.1.call-start = ((), (), s32[]{:S(2)}) async-start(), calls=%async_computation.3 | async-start | bytes 4386816 | tf_op jit(solution)/shard_map/all_gather | solution.py:34
  34.6 142.8 %all-gather.6.cloned.1.call-start = ((), (), s32[]{:S(2)}) async-start(), calls=%async_computation.4 | async-start | bytes 3932160 | tf_op jit(solution)/shard_map/all_gather | solution.py:30
  35.4 215.4 %all-gather.8.cloned.1.call-start = ((), (), s32[]{:S(2)}) async-start(), calls=%async_computation.5 | async-start | bytes 7864320 | tf_op jit(solution)/shard_map/all_gather | solution.py:29
  36.1 305.4 %reduce-scatter.2.cloned.1.call-start = ((), (), s32[]{:S(2)}) async-start(), calls=%async_computation.6 | async-start | bytes 2506752 | tf_op jit(solution)/shard_map/reduce_scatter | solution.py:55
  270.0 91.4 %copy-start = (f32[96,2]{0,1:T(2,128)S(1)}, f32[96,2]{0,1:T(2,128)}, u32[]{:S(2)}) copy-start(f32[96,2]{0,1:T(2,128)} %param.8) | copy-start | bytes 2308
  343.3 26.5 %all-to-all-start.1 = ((bf16[8,42,192]{2,1,0:T(8,128)(2,1)}), bf16[8,42,192]{2,1,0:T(8,128)(2,1)S(1)}, u32[]{:S(2)}, u32[]{:S(2)}) async-start(bf16[8,42,192]{2,1,0:T(8,128)(2,1)} %reshape.34), calls=%async_computation.2 | async-start | bytes 393216 | tf_op jit(solution)/shard_map/all_to_all | solution.py:59
Sparse Core Ops, SparseCore 0:
  34.7 94.8 all-gather.3
  131.7 45.6 all-gather.5
  179.5 71.1 all-gather.7
  270.2 71.3 reduce-scatter.1
where the time goes:
time: 381 us; the launch traced here: 378 us
  waiting for transfers between devices  281 us (74%)
  matrix products  24.6 us (6%)
  blocking collectives  23.5 us (6%)
  starting transfers between devices  18 us (5%)
  local copies, waits for them, and re-layouts  15.2 us (4%)
  between operations  13.2 us (3%)
    all_gather x1, waiting for transfers between devices, body(): piece = lax.all_gather(arrived, 'tensor', axis=1, tiled=True)  93.5 us
    reduce_scatter x1, waiting for transfers between devices, body(): lax.psum_scatter(partial_rows.astype(jnp.bfloat16), 'tensor', scatter_dim...  71.5 us
    all_gather x1, waiting for transfers between devices, body(): lax.all_gather(w_gate_up, 'dp', axis=2, tiled=True)  69.1 us
    all_gather x1, waiting for transfers between devices, body(): lax.all_gather(w_down, 'dp', axis=2, tiled=True)  36.9 us
    all_to_all x1, blocking collectives, body(): lax.all_to_all(outgoing, 'expert', split_axis=0, concat_axis=0, tiled=True)  23.5 us
    all_to_all x1, starting transfers between devices, body(): lax.all_to_all(returned, 'expert', split_axis=0, concat_axis=0, tiled=True)  17.9 us
    dot_general x1, matrix products, body(): lax.dot_general(gate_grad, gate_up[0], contract, preferred_element_type=j...  8.39 us
    all_to_all x1, waiting for transfers between devices, body(): lax.all_to_all(returned, 'expert', split_axis=0, concat_axis=0, tiled=True)  8.26 us
  transfers between devices with their start and end apart: 5, of which 5 were waited for; matrix products, arithmetic and copies ran while one was open for 4% of the time, Pallas kernels for 0%

commit v1 on v0

v1 whole, which is shorter than its diff:
```python
import jax
import jax.numpy as jnp
from jax import lax
from jax.experimental import pallas as pl
from jax.experimental.pallas import tpu as pltpu
from jax.sharding import PartitionSpec as P

MESH = pl.DeviceIdType.MESH
EXPERTS = 8
SLOTS = 42
PAD = 48
WIDTH = 192
PAIR = 384
ROWS = 176
HALF = 1536
SLICE = 768
UNITS = 512
NEAR_RIGHT = 2
NEAR_LEFT = 2
BF = jnp.bfloat16
F32 = jnp.float32


def iota(shape, dim):
    return lax.broadcasted_iota(jnp.int32, shape, dim)


def dot(a, b, ca=1, cb=0):
    return lax.dot_general(a, b, (((ca,), (cb,)), ((), ())), preferred_element_type=F32)


def onehot(mask):
    return mask.astype(F32).astype(BF)


class Copies:
    def __init__(self, send, recv):
        self.send, self.recv = send, recv
        self.sends, self.recvs = 0, 0
        self.pending = []

    def slots(self, count):
        first = self.recvs
        self.recvs += count
        return first

    def make(self, src, dst, device, slot=None):
        if slot is None:
            slot = self.slots(1)
        copy = pltpu.make_async_remote_copy(
            src_ref=src,
            dst_ref=dst,
            send_sem=self.send.at[self.sends],
            recv_sem=self.recv.at[slot],
            device_id=device,
            device_id_type=MESH,
        )
        self.sends += 1
        return copy

    def go(self, src, dst, device, slot=None):
        copy = self.make(src, dst, device, slot)
        copy.start()
        self.pending.append(copy)
        return copy

    def arrived(self, ref, slot):
        pltpu.make_async_copy(ref, ref, self.recv.at[slot]).wait()


SENDS = 160
RECVS = 160


def kernel(
    tokens_ref, grads_ref, gates_ref, ids_ref, wgu_hbm, wd_hbm,
    result_ref,
    outgoing, arrived, block, xg, wgu, wd, part, part_out, part_in, gu, rows_out, rows_in,
    final, final_in, back_out, back, send_sem, recv_sem, local_sem,
):
    e = lax.axis_index("expert")
    t = lax.axis_index("tensor")
    x = lax.axis_index("dp")
    c = lax.rem(e, 2)
    y, z = lax.div(t, 2), lax.rem(t, 2)
    yq = lax.rem(y - 2 * c + 8, 8)
    xq = lax.rem(x - c + 4, 4)
    h = lax.div(xq, 2)
    odd = lax.rem(xq, 2)

    right = {"tensor": 2 * lax.rem(y + 1, 8) + z}
    left = {"tensor": 2 * lax.rem(y + 7, 8) + z}
    across = {"tensor": 2 * y + (1 - z)}
    weights_peer = {"dp": lax.rem(xq + 1 - 2 * odd + c, 4)}
    rows_peer = {"dp": lax.rem(3 - xq + c, 4)}

    def place(core):
        xs = lax.rem(x - core + 4, 4)
        ys = lax.rem(y - 2 * core + 8, 8)
        flip = lax.rem(lax.div(xs, 2) + lax.div(ys, 4), 2)
        x2 = xs + flip * (3 - 2 * xs)
        y2 = ys + flip * (7 - 2 * ys)
        return lax.rem(x2 + core, 4), lax.rem(y2 + 2 * core, 8), flip

    places = [place(0), place(1)]
    px, py, pflip = place(c)
    copies = Copies(send_sem, recv_sem)

    barrier = pltpu.get_barrier_semaphore()
    signals = 0
    for peer in (right, left, across, weights_peer, rows_peer):
        pl.semaphore_signal(barrier, inc=1, device_id=peer, device_id_type=MESH)
        signals += 1
    for other in range(EXPERTS):
        ox, oy, _ = places[other % 2]
        for side in range(2):
            pl.semaphore_signal(
                barrier, inc=1, device_id={"expert": other, "tensor": 2 * oy + side, "dp": ox}, device_id_type=MESH
            )
            pl.semaphore_signal(
                barrier, inc=1, device_id={"expert": other, "tensor": 2 * py + side, "dp": px}, device_id_type=MESH
            )
            signals += 2

    mine = pl.multiple_of(odd * SLICE, SLICE)
    own_gu = pltpu.make_async_copy(wgu_hbm.at[0], wgu.at[:, pl.ds(mine, SLICE), :], local_sem.at[0])
    own_d = pltpu.make_async_copy(wd_hbm.at[0], wd.at[:, pl.ds(mine, SLICE)], local_sem.at[1])
    own_gu.start()
    own_d.start()

    ids = ids_ref[...]
    count = ids.shape[0]
    lanes = iota((count, EXPERTS), 1)
    chosen = [(ids[:, k : k + 1] == lanes).astype(F32) for k in range(2)]
    earlier = onehot(iota((count, count), 1) < iota((count, count), 0))
    before = dot(earlier, (chosen[0] + chosen[1]).astype(BF))
    slot_of = before + (lanes * PAD).astype(F32)
    slot_lanes = iota((count, EXPERTS * PAD), 1)
    picks = []
    for k in range(2):
        target = jnp.sum(chosen[k] * slot_of, axis=1, keepdims=True).astype(jnp.int32)
        picks.append((target == slot_lanes).astype(F32))
    select = (picks[0] + picks[1]).astype(BF)
    for kind, source in enumerate((tokens_ref, grads_ref)):
        chosen_rows = dot(select, source[...], 0, 0).astype(BF)
        outgoing[kind] = chosen_rows.reshape(EXPERTS, PAD, WIDTH)

    pl.semaphore_wait(barrier, signals)

    base = copies.slots(2 * EXPERTS)
    to_self = []
    for other in range(EXPERTS):
        ox, oy, oflip = places[other % 2]
        for kind in range(2):
            target = {"expert": other, "tensor": 2 * oy + kind, "dp": ox}
            slot = base + 2 * e + z
            copy = copies.make(outgoing.at[kind, other], arrived.at[e, z], target, slot)
            stays = jnp.logical_and(jnp.logical_and(e == other, z == kind), oflip == 0)
            here = pltpu.make_async_copy(outgoing.at[kind, other], arrived.at[e, z], recv_sem.at[slot])
            pl.when(stays)(here.start)
            pl.when(jnp.logical_not(stays))(copy.start)
            to_self.append((stays, copy))

    w1 = copies.go(wgu_hbm.at[0], wgu.at[:, pl.ds(mine, SLICE), :], weights_peer)
    w2 = copies.go(wd_hbm.at[0], wd.at[:, pl.ds(mine, SLICE)], weights_peer)

    embed = [onehot(iota((WIDTH, PAIR), 1) == iota((WIDTH, PAIR), 0) + WIDTH * side) for side in range(2)]
    dense = iota((ROWS, 4 * PAD), 0)
    padded = dense + (PAD - SLOTS) * sum((dense >= SLOTS * n).astype(jnp.int32) for n in range(1, 4))
    pack = onehot(jnp.logical_and(padded == iota((ROWS, 4 * PAD), 1), dense < 4 * SLOTS))

    def holds(origin):
        r = lax.div(origin, 4)
        same = 1 - lax.rem(r + h, 2)
        source = origin + (1 - same) * (7 - 2 * origin)
        return r, source - 4 * h

    def spot(n, kind, origin):
        r, pair = holds(origin)
        return xg.at[n, kind, r, :, pl.ds(pl.multiple_of(pair * PAIR, PAIR), PAIR)]

    def repack(n):
        for side in range(2):
            for source in range(4):
                copies.arrived(arrived.at[4 * n + source, side], base + 2 * (4 * n + source) + side)
        wide = sum(dot(arrived[4 * n : 4 * n + 4, side].reshape(4 * PAD, WIDTH), embed[side]) for side in range(2))
        block[n] = dot(pack, wide.astype(BF)).astype(BF)

    def gather(n):
        here = pltpu.make_async_copy(block.at[n], spot(n, z, yq), local_sem.at[2 + n])
        here.start()
        swap = copies.go(block.at[n], spot(n, z, yq), across)
        moves = {}

        def origin(way, step):
            return lax.rem(yq - step + 8, 8) if way == 0 else lax.rem(yq + step, 8)

        def push(way, kind, step, source=None):
            side = z if kind == 0 else 1 - z
            ref = spot(n, side, origin(way, step - 1))
            moves[way, kind, step] = copies.go(source if source is not None else ref, ref, right if way == 0 else left)

        reach = {(0, 0): 4, (1, 0): 3, (0, 1): NEAR_RIGHT, (1, 1): NEAR_LEFT}
        far = []
        push(0, 0, 1, block.at[n])
        push(1, 0, 1, block.at[n])
        yield
        swap.wait_recv()
        push(0, 1, 1)
        push(1, 1, 1)
        yield
        for step in range(1, 5):
            for way in range(2):
                if step > reach[way, 0]:
                    continue
                moves[way, 0, step].wait_recv()
                if step < reach[way, 0]:
                    push(way, 0, step + 1)
                if step > reach[way, 1]:
                    ref = spot(n, z, origin(way, step))
                    far.append(copies.go(ref, ref, across))
            yield
            for way in range(2):
                if step > reach[way, 1]:
                    continue
                moves[way, 1, step].wait_recv()
                if step < reach[way, 1]:
                    push(way, 1, step + 1)
            yield
        for copy in far:
            copy.wait_recv()
        here.wait()

    exchange = {}

    def forward(n):
        for which in range(3):
            data = xg[n, 1 if which == 2 else 0].reshape(2 * ROWS, HALF)
            if which < 2:
                value = dot(data, wgu[which])
            else:
                value = dot(data, wd[...], 1, 1)
            part[n, which] = value
            part_out[n, which] = value.astype(BF)
            exchange[n, which] = copies.go(part_out.at[n, which], part_in.at[n, which], rows_peer)
            yield

    def middle(n):
        for which in range(3):
            exchange[n, which].wait_recv()
        for r in range(2):
            span = pl.ds(r * ROWS, ROWS)
            gate, up, hidden = (part[n, w, span, :] + part_in[n, w, span, :].astype(F32) for w in range(3))
            sigma = jax.nn.sigmoid(gate)
            gu[n, r, :, :UNITS] = (hidden * up * sigma * (1.0 + gate * (1.0 - sigma))).astype(BF)
            gu[n, r, :, UNITS:] = (hidden * gate * sigma).astype(BF)
            yield

    def backward(n):
        def product(away):
            r, pair = holds(lax.rem(yq + away + 8, 8))
            span = pl.ds(pl.multiple_of(pair * PAIR, PAIR), PAIR)
            value = dot(gu[n, r, :, :UNITS], wgu[0, span, :], 1, 1)
            value = value + dot(gu[n, r, :, UNITS:], wgu[1, span, :], 1, 1)
            return value

        moves = {}
        chains = ((0, right, (4, 3, 2, 1)), (4, left, (-3, -2, -1)))
        for step in range(4):
            for first, way, aways in chains:
                if step >= len(aways):
                    continue
                index = first + step
                value = product(aways[step])
                if step > 0:
                    moves[index - 1].wait_recv()
                    value = value + rows_in[n, index - 1].astype(F32)
                rows_out[n, index] = value.astype(BF)
                moves[index] = copies.go(rows_out.at[n, index], rows_in.at[n, index], way)
            yield
        value = product(0)
        for last in (6, 3):
            moves[last].wait_recv()
            value = value + rows_in[n, last].astype(F32)
        final[n] = value
        yield

    def run(*work):
        for steps in work:
            for _ in steps:
                pass

    def advance(steps, times=1):
        for _ in range(times):
            next(steps, None)

    repack(0)
    gather_a = gather(0)
    advance(gather_a)
    repack(1)
    gather_b = gather(1)
    advance(gather_a, 3)
    advance(gather_b)
    run(gather_a)
    own_gu.wait()
    own_d.wait()
    w1.wait_recv()
    w2.wait_recv()
    advance(gather_b)
    for _ in forward(0):
        advance(gather_b, 2)
    run(gather_b)
    run(forward(1))
    run(middle(0))
    run(backward(0))
    run(middle(1))
    run(backward(1))

    final_out = final_in.at[1]
    final_in[1] = final[1 - z].astype(BF)
    cross = copies.go(final_out, final_in.at[0], across)
    cross.wait_recv()
    total = (final[z] + final_in[0].astype(F32)).astype(BF)
    unpacked = dot(pack, total, 0, 0).astype(BF)
    for side in range(2):
        back_out[side] = dot(unpacked, embed[side], 1, 1).astype(BF).reshape(4, PAD, WIDTH)

    base_back = copies.slots(EXPERTS)
    for source in range(4):
        for side in range(2):
            owner = 4 * z + source
            slot = base_back + e
            copy = copies.make(
                back_out.at[side, source], back.at[e], {"expert": owner, "tensor": 2 * py + side, "dp": px}, slot
            )
            stays = jnp.logical_and(jnp.logical_and(e == owner, z == side), pflip == 0)
            here = pltpu.make_async_copy(back_out.at[side, source], back.at[e], recv_sem.at[slot])
            pl.when(stays)(here.start)
            pl.when(jnp.logical_not(stays))(copy.start)
            to_self.append((stays, copy))
    for other in range(EXPERTS):
        copies.arrived(back.at[other], base_back + other)

    returned = back[...].reshape(EXPERTS * PAD, WIDTH)
    gates = gates_ref[...]
    total = jnp.zeros((count, WIDTH), F32)
    for k in range(2):
        total = total + gates[:, k : k + 1] * dot(picks[k].astype(BF), returned)
    result_ref[...] = total.astype(BF)

    for copy in copies.pending:
        copy.wait_send()
    for stays, copy in to_self:
        pl.when(jnp.logical_not(stays))(copy.wait_send)
    assert copies.sends <= SENDS and copies.recvs <= RECVS


def body(tokens, out_grad, gates, expert_ids, w_gate_up, w_down):
    vmem = pl.BlockSpec(memory_space=pltpu.VMEM)
    hbm = pl.BlockSpec(memory_space=pl.ANY)
    return pl.pallas_call(
        kernel,
        out_shape=jax.ShapeDtypeStruct(tokens.shape, BF),
        in_specs=[vmem, vmem, vmem, vmem, hbm, hbm],
        out_specs=vmem,
        scratch_shapes=[
            pltpu.VMEM((2, EXPERTS, PAD, WIDTH), BF),
            pltpu.VMEM((EXPERTS, 2, PAD, WIDTH), BF),
            pltpu.VMEM((2, ROWS, PAIR), BF),
            pltpu.VMEM((2, 2, 2, ROWS, HALF), BF),
            pltpu.VMEM((2, HALF, UNITS), BF),
            pltpu.VMEM((UNITS, HALF), BF),
            pltpu.VMEM((2, 3, 2 * ROWS, UNITS), F32),
            pltpu.VMEM((2, 3, 2 * ROWS, UNITS), BF),
            pltpu.VMEM((2, 3, 2 * ROWS, UNITS), BF),
            pltpu.VMEM((2, 2, ROWS, 2 * UNITS), BF),
            pltpu.VMEM((2, 7, ROWS, PAIR), BF),
            pltpu.VMEM((2, 7, ROWS, PAIR), BF),
            pltpu.VMEM((2, ROWS, PAIR), F32),
            pltpu.VMEM((2, ROWS, PAIR), BF),
            pltpu.VMEM((2, 4, PAD, WIDTH), BF),
            pltpu.VMEM((EXPERTS, PAD, WIDTH), BF),
            pltpu.SemaphoreType.DMA((SENDS,)),
            pltpu.SemaphoreType.DMA((RECVS,)),
            pltpu.SemaphoreType.DMA((4,)),
        ],
        compiler_params=pltpu.CompilerParams(
            collective_id=0, has_side_effects=True, vmem_limit_bytes=56 * 1024 * 1024
        ),
    )(tokens, out_grad, gates, expert_ids, w_gate_up, w_down)


def solution(mesh):
    return jax.shard_map(
        body,
        mesh=mesh,
        in_specs=(
            P(("expert", "dp"), "tensor"),
            P(("expert", "dp"), "tensor"),
            P(("expert", "dp"), None),
            P(("expert", "dp"), None),
            P("expert", None, "dp", "tensor"),
            P("expert", "tensor", "dp"),
        ),
        out_specs=P(("expert", "dp"), "tensor"),
        check_vma=False,
    )
```

time: 381 us -> 153 us (0.40)
  waiting for transfers between devices: 281 us -> 0 us
  Pallas kernels: 0 us -> 149 us
  matrix products: 24.6 us -> 0 us
  blocking collectives: 23.5 us -> 0 us
  starting transfers between devices: 18 us -> 0 us
  between operations: 13.2 us -> 0.01 us
  local copies, waits for them, and re-layouts: 15.2 us -> 4.21 us
    all_gather x3 -> x0, waiting for transfers between devices: 199 us -> none  [the longest x1 93.5 us: body(): piece = lax.all_gather(arrived, 'tensor', axis=1, tiled=True)]
    pallas_call x0 -> x1, Pallas kernels: none -> 149 us  [body(): pl.pallas_call(kernel, out_shape=jax.ShapeDtypeStruct(tokens.shape, BF),...]
    reduce_scatter x1 -> x0, waiting for transfers between devices: 71.5 us -> none  [body(): lax.psum_scatter(partial_rows.astype(jnp.bfloat16), 'tensor', scatter_dim...]
    dot_general x5 -> x0, matrix products: 24.6 us -> none  [the longest x1 8.39 us: body(): lax.dot_general(gate_grad, gate_up[0], contract, preferred_element_type=j...]
    all_to_all x1 -> x0, blocking collectives: 23.5 us -> none  [body(): lax.all_to_all(outgoing, 'expert', split_axis=0, concat_axis=0, tiled=True)]
    all_to_all x1 -> x0, starting transfers between devices: 17.9 us -> none  [body(): lax.all_to_all(returned, 'expert', split_axis=0, concat_axis=0, tiled=True)]
    all_to_all x1 -> x0, waiting for transfers between devices: 8.26 us -> none  [body(): lax.all_to_all(returned, 'expert', split_axis=0, concat_axis=0, tiled=True)]
    all_gather x1 -> x0, local copies, waits for them, and re-layouts: 6.53 us -> none  [body(): piece = lax.all_gather(arrived, 'tensor', axis=1, tiled=True)]
  transfers between devices with their start and end apart: 5 -> 0, of which waited for: 5 -> 0; matrix products, arithmetic and copies ran while one was open for 4% -> 0% of each run, Pallas kernels for 0% -> 0%
where the time goes in v1:
time: 153 us
  Pallas kernels  149 us (97%)
  local copies, waits for them, and re-layouts  4.21 us (3%)
    pallas_call x1, Pallas kernels, body(): pl.pallas_call(kernel, out_shape=jax.ShapeDtypeStruct(tokens.shape, BF),...  149 us
    unnamed x3, local copies, waits for them, and re-layouts  4.21 us

profile of v1, /device:TPU:7, one launch (start us, length us, event | category | flops | bytes accessed | tf_op | source)
XLA Modules:
  0.0 153.0 jit_solution(10462042577905339688)
XLA Ops:
  0.0 1.4 copy.7.gates_ref
  1.4 1.4 copy.8.ids_ref
  2.8 148.8 %shard_map.64 = bf16[96,192]{1,0:T(8,128)(2,1)} custom-call(bf16[96,192]{1,0:T(8,128)(2,1)} %tokens_ref.1, bf16[96,192]{1,0:T(8,128)(2,1)} %grads_ref.1, f32[96,2]{1,0:T(8,128)} %copy.7.gates_ref, s32[96,2]{1,0:T(8,128)} %copy.8.ids_ref, bf16[1,2,768,512]{3,2,1,0:T(8,128)(2,1)} %wgu_hbm.1, bf16[1,512,768]{2,1,0:T(8,128)(2,1)} %wd_hbm.1), custom_call_target="tpu_custom_call" | custom-call | tf_op jit(solution)/shard_map/pallas_call | solution.py:361
  151.6 1.4 copy.10

commit v2 on v1

--- a/solution.py
+++ b/solution.py
@@ -15,8 +15,9 @@
 HALF = 1536
 SLICE = 768
 UNITS = 512
-NEAR_RIGHT = 2
+NEAR_RIGHT = 1
 NEAR_LEFT = 2
+ORDER = (4, 5, 3, 2, 6, 1, 7, 0)
 BF = jnp.bfloat16
 F32 = jnp.float32
 
@@ -75,7 +76,7 @@
 def kernel(
     tokens_ref, grads_ref, gates_ref, ids_ref, wgu_hbm, wd_hbm,
     result_ref,
-    outgoing, arrived, block, xg, wgu, wd, part, part_out, part_in, gu, rows_out, rows_in,
+    outgoing, arrived, packed, block, xg, wgu, wd, part, part_out, part_in, gu, rows_out, rows_in,
     final, final_in, back_out, back, send_sem, recv_sem, local_sem,
 ):
     e = lax.axis_index("expert")
@@ -99,28 +100,24 @@
         ys = lax.rem(y - 2 * core + 8, 8)
         flip = lax.rem(lax.div(xs, 2) + lax.div(ys, 4), 2)
         x2 = xs + flip * (3 - 2 * xs)
-        y2 = ys + flip * (7 - 2 * ys)
+        y2 = ys + flip * (6 + 2 * lax.rem(ys, 2) - 2 * ys)
         return lax.rem(x2 + core, 4), lax.rem(y2 + 2 * core, 8), flip
 
-    places = [place(0), place(1)]
     px, py, pflip = place(c)
+    mirror = {"tensor": 2 * py + z, "dp": px}
     copies = Copies(send_sem, recv_sem)
 
     barrier = pltpu.get_barrier_semaphore()
     signals = 0
-    for peer in (right, left, across, weights_peer, rows_peer):
+    for peer in (right, left, across, weights_peer, rows_peer, mirror):
         pl.semaphore_signal(barrier, inc=1, device_id=peer, device_id_type=MESH)
         signals += 1
     for other in range(EXPERTS):
-        ox, oy, _ = places[other % 2]
         for side in range(2):
             pl.semaphore_signal(
-                barrier, inc=1, device_id={"expert": other, "tensor": 2 * oy + side, "dp": ox}, device_id_type=MESH
+                barrier, inc=1, device_id={"expert": other, "tensor": 2 * y + side}, device_id_type=MESH
             )
-            pl.semaphore_signal(
-                barrier, inc=1, device_id={"expert": other, "tensor": 2 * py + side, "dp": px}, device_id_type=MESH
-            )
-            signals += 2
+            signals += 1
 
     mine = pl.multiple_of(odd * SLICE, SLICE)
     own_gu = pltpu.make_async_copy(wgu_hbm.at[0], wgu.at[:, pl.ds(mine, SLICE), :], local_sem.at[0])
@@ -129,33 +126,37 @@
     own_d.start()
 
     ids = ids_ref[...]
-    count = ids.shape[0]
-    lanes = iota((count, EXPERTS), 1)
-    chosen = [(ids[:, k : k + 1] == lanes).astype(F32) for k in range(2)]
-    earlier = onehot(iota((count, count), 1) < iota((count, count), 0))
-    before = dot(earlier, (chosen[0] + chosen[1]).astype(BF))
-    slot_of = before + (lanes * PAD).astype(F32)
-    slot_lanes = iota((count, EXPERTS * PAD), 1)
+    count = ids.shape[1]
+    lines = iota((EXPERTS, count), 0)
+    chosen = [(ids[k : k + 1, :] == lines).astype(F32) for k in range(2)]
+    earlier = onehot(iota((count, count), 0) < iota((count, count), 1))
+    before = dot((chosen[0] + chosen[1]).astype(BF), earlier)
+    slot_of = before + (lines * PAD).astype(F32)
+    slot_lines = iota((EXPERTS * PAD, count), 0)
     picks = []
     for k in range(2):
-        target = jnp.sum(chosen[k] * slot_of, axis=1, keepdims=True).astype(jnp.int32)
-        picks.append((target == slot_lanes).astype(F32))
+        target = jnp.sum(chosen[k] * slot_of, axis=0, keepdims=True).astype(jnp.int32)
+        picks.append((target == slot_lines).astype(F32))
     select = (picks[0] + picks[1]).astype(BF)
     for kind, source in enumerate((tokens_ref, grads_ref)):
-        chosen_rows = dot(select, source[...], 0, 0).astype(BF)
+        chosen_rows = dot(select, source[...]).astype(BF)
         outgoing[kind] = chosen_rows.reshape(EXPERTS, PAD, WIDTH)
 
     pl.semaphore_wait(barrier, signals)
 
     base = copies.slots(2 * EXPERTS)
     to_self = []
-    for other in range(EXPERTS):
-        ox, oy, oflip = places[other % 2]
+    for turn in ORDER:
+        other = lax.rem(e + turn, EXPERTS)
         for kind in range(2):
-            target = {"expert": other, "tensor": 2 * oy + kind, "dp": ox}
+            target = {"expert": other, "tensor": 2 * y + kind}
             slot = base + 2 * e + z
             copy = copies.make(outgoing.at[kind, other], arrived.at[e, z], target, slot)
-            stays = jnp.logical_and(jnp.logical_and(e == other, z == kind), oflip == 0)
+            if turn:
+                copy.start()
+                copies.pending.append(copy)
+                continue
+            stays = z == kind
             here = pltpu.make_async_copy(outgoing.at[kind, other], arrived.at[e, z], recv_sem.at[slot])
             pl.when(stays)(here.start)
             pl.when(jnp.logical_not(stays))(copy.start)
@@ -172,7 +173,7 @@
     def holds(origin):
         r = lax.div(origin, 4)
         same = 1 - lax.rem(r + h, 2)
-        source = origin + (1 - same) * (7 - 2 * origin)
+        source = origin + (1 - same) * (6 + 2 * lax.rem(origin, 2) - 2 * origin)
         return r, source - 4 * h
 
     def spot(n, kind, origin):
@@ -184,52 +185,61 @@
             for source in range(4):
                 copies.arrived(arrived.at[4 * n + source, side], base + 2 * (4 * n + source) + side)
         wide = sum(dot(arrived[4 * n : 4 * n + 4, side].reshape(4 * PAD, WIDTH), embed[side]) for side in range(2))
-        block[n] = dot(pack, wide.astype(BF)).astype(BF)
-
-    def gather(n):
-        here = pltpu.make_async_copy(block.at[n], spot(n, z, yq), local_sem.at[2 + n])
-        here.start()
-        swap = copies.go(block.at[n], spot(n, z, yq), across)
-        moves = {}
-
-        def origin(way, step):
+        packed[n] = dot(pack, wide.astype(BF)).astype(BF)
+        copy = copies.make(packed.at[n], block.at[n], mirror)
+        here = pltpu.make_async_copy(packed.at[n], block.at[n], recv_sem.at[copies.recvs - 1])
+        pl.when(pflip == 0)(here.start)
+        pl.when(pflip == 1)(copy.start)
+        to_self.append((pflip == 0, copy))
+        return here
+
+    class Gather:
+        reach = {(0, 0): 4, (1, 0): 3, (0, 1): NEAR_RIGHT, (1, 1): NEAR_LEFT}
+
+        def __init__(self, n):
+            self.n = n
+            self.moves = {}
+            self.far = []
+            self.here = pltpu.make_async_copy(block.at[n], spot(n, z, yq), local_sem.at[2 + n])
+            self.here.start()
+            self.push(0, 0, 1, block.at[n])
+            self.push(1, 0, 1, block.at[n])
+            self.swap = copies.go(block.at[n], spot(n, z, yq), across)
+
+        def origin(self, way, step):
             return lax.rem(yq - step + 8, 8) if way == 0 else lax.rem(yq + step, 8)
 
-        def push(way, kind, step, source=None):
+        def push(self, way, kind, step, source=None):
             side = z if kind == 0 else 1 - z
-            ref = spot(n, side, origin(way, step - 1))
-            moves[way, kind, step] = copies.go(source if source is not None else ref, ref, right if way == 0 else left)
-
-        reach = {(0, 0): 4, (1, 0): 3, (0, 1): NEAR_RIGHT, (1, 1): NEAR_LEFT}
-        far = []
-        push(0, 0, 1, block.at[n])
-        push(1, 0, 1, block.at[n])
-        yield
-        swap.wait_recv()
-        push(0, 1, 1)
-        push(1, 1, 1)
-        yield
-        for step in range(1, 5):
+            ref = spot(self.n, side, self.origin(way, step - 1))
+            self.moves[way, kind, step] = copies.go(ref if source is None else source, ref, right if way == 0 else left)
+
+        def swapped(self):
+            self.swap.wait_recv()
+            self.push(0, 1, 1)
+            self.push(1, 1, 1)
+
+        def own(self, step):
             for way in range(2):
-                if step > reach[way, 0]:
-                    continue
-                moves[way, 0, step].wait_recv()
-                if step < reach[way, 0]:
-                    push(way, 0, step + 1)
-                if step > reach[way, 1]:
-                    ref = spot(n, z, origin(way, step))
-                    far.append(copies.go(ref, ref, across))
-            yield
+                if step <= self.reach[way, 0]:
+                    self.moves[way, 0, step].wait_recv()
+                    if step < self.reach[way, 0]:
+                        self.push(way, 0, step + 1)
+                    if step > self.reach[way, 1]:
+                        ref = spot(self.n, z, self.origin(way, step))
+                        self.far.append(copies.go(ref, ref, across))
+
+        def other(self, step):
             for way in range(2):
-                if step > reach[way, 1]:
-                    continue
-                moves[way, 1, step].wait_recv()
-                if step < reach[way, 1]:
-                    push(way, 1, step + 1)
-            yield
-        for copy in far:
-            copy.wait_recv()
-        here.wait()
+                if step <= self.reach[way, 1]:
+                    self.moves[way, 1, step].wait_recv()
+                    if step < self.reach[way, 1]:
+                        self.push(way, 1, step + 1)
+
+        def finish(self):
+            for copy in self.far:
+                copy.wait_recv()
+            self.here.wait()
 
     exchange = {}
 
@@ -294,27 +304,46 @@
         for _ in range(times):
             next(steps, None)
 
-    repack(0)
-    gather_a = gather(0)
-    advance(gather_a)
-    repack(1)
-    gather_b = gather(1)
-    advance(gather_a, 3)
-    advance(gather_b)
-    run(gather_a)
+    swap_a = repack(0)
+    swap_b = repack(1)
+    swap_a.wait()
+    ga = Gather(0)
+    swap_b.wait()
+    gb = Gather(1)
+    ga.own(1)
+    ga.swapped()
+    ga.own(2)
+    ga.other(1)
+    ga.own(3)
+    gb.own(1)
+    gb.swapped()
+    ga.own(4)
+    ga.other(2)
+    gb.own(2)
+    gb.other(1)
+    ga.finish()
     own_gu.wait()
     own_d.wait()
     w1.wait_recv()
     w2.wait_recv()
-    advance(gather_b)
-    for _ in forward(0):
-        advance(gather_b, 2)
-    run(gather_b)
+    fa = forward(0)
+    advance(fa)
+    gb.own(3)
+    gb.other(2)
+    run(fa)
+    gb.own(4)
+    gb.finish()
     run(forward(1))
     run(middle(0))
-    run(backward(0))
+    ba = backward(0)
+    advance(ba, 3)
     run(middle(1))
-    run(backward(1))
+    bb = backward(1)
+    advance(bb)
+    advance(ba)
+    advance(bb)
+    advance(ba)
+    run(bb)
 
     final_out = final_in.at[1]
     final_in[1] = final[1 - z].astype(BF)
@@ -326,9 +355,10 @@
         back_out[side] = dot(unpacked, embed[side], 1, 1).astype(BF).reshape(4, PAD, WIDTH)
 
     base_back = copies.slots(EXPERTS)
-    for source in range(4):
+    for turn in (2, 3, 1, 0):
+        source = lax.rem(e + turn, 4)
+        owner = 4 * z + source
         for side in range(2):
-            owner = 4 * z + source
             slot = base_back + e
             copy = copies.make(
                 back_out.at[side, source], back.at[e], {"expert": owner, "tensor": 2 * py + side, "dp": px}, slot
@@ -343,9 +373,11 @@
 
     returned = back[...].reshape(EXPERTS * PAD, WIDTH)
     gates = gates_ref[...]
+    diagonal = iota((count, count), 0) == iota((count, count), 1)
     total = jnp.zeros((count, WIDTH), F32)
     for k in range(2):
-        total = total + gates[:, k : k + 1] * dot(picks[k].astype(BF), returned)
+        gate = jnp.sum(jnp.where(diagonal, gates[k : k + 1, :], 0.0), axis=1, keepdims=True)
+        total = total + gate * dot(picks[k].astype(BF), returned, 0, 0)
     result_ref[...] = total.astype(BF)
 
     for copy in copies.pending:
@@ -366,6 +398,7 @@
         scratch_shapes=[
             pltpu.VMEM((2, EXPERTS, PAD, WIDTH), BF),
             pltpu.VMEM((EXPERTS, 2, PAD, WIDTH), BF),
+            pltpu.VMEM((2, ROWS, PAIR), BF),
             pltpu.VMEM((2, ROWS, PAIR), BF),
             pltpu.VMEM((2, 2, 2, ROWS, HALF), BF),
             pltpu.VMEM((2, HALF, UNITS), BF),
@@ -387,7 +420,7 @@
         compiler_params=pltpu.CompilerParams(
             collective_id=0, has_side_effects=True, vmem_limit_bytes=56 * 1024 * 1024
         ),
-    )(tokens, out_grad, gates, expert_ids, w_gate_up, w_down)
+    )(tokens, out_grad, gates.T, expert_ids.T, w_gate_up, w_down)
 
 
 def solution(mesh):

time: 153 us -> 130 us (0.85); the launches traced: 153 us -> 128 us
  Pallas kernels: 149 us -> 127 us
  local copies, waits for them, and re-layouts: 4.21 us -> 1.42 us
    pallas_call x1, Pallas kernels: 149 us -> 127 us  [body(): pl.pallas_call(kernel, out_shape=jax.ShapeDtypeStruct(tokens.shape, BF),...]
    unnamed x3 -> x1, local copies, waits for them, and re-layouts: 4.21 us -> 1.42 us
where the time goes in v2:
time: 130 us; the launch traced here: 128 us
  Pallas kernels  127 us (98%)
  local copies, waits for them, and re-layouts  1.42 us (1%)
    pallas_call x1, Pallas kernels, body(): pl.pallas_call(kernel, out_shape=jax.ShapeDtypeStruct(tokens.shape, BF),...  127 us

profile of v2, /device:TPU:7, one launch (start us, length us, event | category | flops | bytes accessed | tf_op | source)
XLA Modules:
  0.0 128.2 jit_solution(6912371853326214853)
XLA Ops:
  0.0 126.8 %shard_map.64 = bf16[96,192]{1,0:T(8,128)(2,1)} custom-call(bf16[96,192]{1,0:T(8,128)(2,1)} %tokens_ref.1, bf16[96,192]{1,0:T(8,128)(2,1)} %grads_ref.1, f32[2,96]{1,0:T(2,128)} %bitcast.2, s32[2,96]{1,0:T(2,128)} %bitcast.3, bf16[1,2,768,512]{3,2,1,0:T(8,128)(2,1)} %wgu_hbm.1, bf16[1,512,768]{2,1,0:T(8,128)(2,1)} %wd_hbm.1), custom_call_target="tpu_custom_call" | custom-call | tf_op jit(solution)/shard_map/pallas_call | solution.py:393
  126.8 1.4 %copy.8 = bf16[96,192]{1,0:T(8,128)(2,1)} copy(bf16[96,192]{1,0:T(8,128)(2,1)} %shard_map.64) | data formatting | bytes 73728

commit v3 on v2

--- a/solution.py
+++ b/solution.py
@@ -76,8 +76,8 @@
 def kernel(
     tokens_ref, grads_ref, gates_ref, ids_ref, wgu_hbm, wd_hbm,
     result_ref,
-    outgoing, arrived, packed, block, xg, wgu, wd, part, part_out, part_in, gu, rows_out, rows_in,
-    final, final_in, back_out, back, send_sem, recv_sem, local_sem,
+    outgoing, arrived, packed, block, xg, wgu, wd, part, part_out, part_in, gu, products, swapped,
+    rows_out, rows_in, back_out, back, send_sem, recv_sem, local_sem,
 ):
     e = lax.axis_index("expert")
     t = lax.axis_index("tensor")
@@ -262,37 +262,72 @@
             span = pl.ds(r * ROWS, ROWS)
             gate, up, hidden = (part[n, w, span, :] + part_in[n, w, span, :].astype(F32) for w in range(3))
             sigma = jax.nn.sigmoid(gate)
-            gu[n, r, :, :UNITS] = (hidden * up * sigma * (1.0 + gate * (1.0 - sigma))).astype(BF)
-            gu[n, r, :, UNITS:] = (hidden * gate * sigma).astype(BF)
+            gate_grad = (hidden * up * sigma * (1.0 + gate * (1.0 - sigma))).astype(BF)
+            up_grad = (hidden * gate * sigma).astype(BF)
+            gu[n, r, :, :UNITS] = dot(pack, gate_grad, 0, 0).astype(BF)
+            gu[n, r, :, UNITS:] = dot(pack, up_grad, 0, 0).astype(BF)
             yield
 
+    back_base = copies.slots(EXPERTS)
+
     def backward(n):
-        def product(away):
-            r, pair = holds(lax.rem(yq + away + 8, 8))
+        aways = (4, 3, 2, 1, -3, -2, -1, 0)
+        swaps, moves = {}, {}
+
+        def product(index):
+            r, pair = holds(lax.rem(yq + aways[index] + 8, 8))
             span = pl.ds(pl.multiple_of(pair * PAIR, PAIR), PAIR)
             value = dot(gu[n, r, :, :UNITS], wgu[0, span, :], 1, 1)
             value = value + dot(gu[n, r, :, UNITS:], wgu[1, span, :], 1, 1)
-            return value
-
-        moves = {}
-        chains = ((0, right, (4, 3, 2, 1)), (4, left, (-3, -2, -1)))
-        for step in range(4):
-            for first, way, aways in chains:
-                if step >= len(aways):
-                    continue
-                index = first + step
-                value = product(aways[step])
-                if step > 0:
-                    moves[index - 1].wait_recv()
-                    value = value + rows_in[n, index - 1].astype(F32)
-                rows_out[n, index] = value.astype(BF)
-                moves[index] = copies.go(rows_out.at[n, index], rows_in.at[n, index], way)
-            yield
-        value = product(0)
+            products[n, index] = value.astype(BF).reshape(2, 2 * PAD, PAIR)
+            swaps[index] = copies.go(products.at[n, index, 1 - z], swapped.at[n, index], across)
+
+        def mine(index):
+            swaps[index].wait_recv()
+            return products[n, index, z].astype(F32) + swapped[n, index].astype(F32)
+
+        def link(index, way, first):
+            value = mine(index)
+            if not first:
+                moves[index - 1].wait_recv()
+                value = value + rows_in[n, index - 1].astype(F32)
+            rows_out[n, index] = value.astype(BF)
+            moves[index] = copies.go(rows_out.at[n, index], rows_in.at[n, index], way)
+
+        for index in (0, 4, 1, 5):
+            product(index)
+        link(0, right, True)
+        link(4, left, True)
+        for index in (2, 6, 3, 7):
+            product(index)
+        yield
+        link(1, right, False)
+        link(5, left, False)
+        yield
+        link(2, right, False)
+        link(6, left, False)
+        yield
+        link(3, right, False)
+        yield
+        value = mine(7)
         for last in (6, 3):
             moves[last].wait_recv()
             value = value + rows_in[n, last].astype(F32)
-        final[n] = value
+        total = value.astype(BF)
+        for side in range(2):
+            back_out[n, side] = dot(total, embed[side], 1, 1).astype(BF).reshape(2, PAD, WIDTH)
+        for turn in range(2):
+            source = lax.rem(e + turn, 2)
+            owner = 4 * n + 2 * z + source
+            for side in range(2):
+                slot = back_base + e
+                target = {"expert": owner, "tensor": 2 * py + side, "dp": px}
+                copy = copies.make(back_out.at[n, side, source], back.at[e], target, slot)
+                stays = jnp.logical_and(jnp.logical_and(e == owner, z == side), pflip == 0)
+                here = pltpu.make_async_copy(back_out.at[n, side, source], back.at[e], recv_sem.at[slot])
+                pl.when(stays)(here.start)
+                pl.when(jnp.logical_not(stays))(copy.start)
+                to_self.append((stays, copy))
         yield
 
     def run(*work):
@@ -336,40 +371,15 @@
     run(forward(1))
     run(middle(0))
     ba = backward(0)
-    advance(ba, 3)
+    advance(ba, 2)
     run(middle(1))
     bb = backward(1)
-    advance(bb)
-    advance(ba)
-    advance(bb)
-    advance(ba)
+    for _ in range(3):
+        advance(bb)
+        advance(ba)
     run(bb)
-
-    final_out = final_in.at[1]
-    final_in[1] = final[1 - z].astype(BF)
-    cross = copies.go(final_out, final_in.at[0], across)
-    cross.wait_recv()
-    total = (final[z] + final_in[0].astype(F32)).astype(BF)
-    unpacked = dot(pack, total, 0, 0).astype(BF)
-    for side in range(2):
-        back_out[side] = dot(unpacked, embed[side], 1, 1).astype(BF).reshape(4, PAD, WIDTH)
-
-    base_back = copies.slots(EXPERTS)
-    for turn in (2, 3, 1, 0):
-        source = lax.rem(e + turn, 4)
-        owner = 4 * z + source
-        for side in range(2):
-            slot = base_back + e
-            copy = copies.make(
-                back_out.at[side, source], back.at[e], {"expert": owner, "tensor": 2 * py + side, "dp": px}, slot
-            )
-            stays = jnp.logical_and(jnp.logical_and(e == owner, z == side), pflip == 0)
-            here = pltpu.make_async_copy(back_out.at[side, source], back.at[e], recv_sem.at[slot])
-            pl.when(stays)(here.start)
-            pl.when(jnp.logical_not(stays))(copy.start)
-            to_self.append((stays, copy))
     for other in range(EXPERTS):
-        copies.arrived(back.at[other], base_back + other)
+        copies.arrived(back.at[other], back_base + other)
 
     returned = back[...].reshape(EXPERTS * PAD, WIDTH)
     gates = gates_ref[...]
@@ -406,12 +416,12 @@
             pltpu.VMEM((2, 3, 2 * ROWS, UNITS), F32),
             pltpu.VMEM((2, 3, 2 * ROWS, UNITS), BF),
             pltpu.VMEM((2, 3, 2 * ROWS, UNITS), BF),
-            pltpu.VMEM((2, 2, ROWS, 2 * UNITS), BF),
-            pltpu.VMEM((2, 7, ROWS, PAIR), BF),
-            pltpu.VMEM((2, 7, ROWS, PAIR), BF),
-            pltpu.VMEM((2, ROWS, PAIR), F32),
-            pltpu.VMEM((2, ROWS, PAIR), BF),
-            pltpu.VMEM((2, 4, PAD, WIDTH), BF),
+            pltpu.VMEM((2, 2, 4 * PAD, 2 * UNITS), BF),
+            pltpu.VMEM((2, 8, 2, 2 * PAD, PAIR), BF),
+            pltpu.VMEM((2, 8, 2 * PAD, PAIR), BF),
+            pltpu.VMEM((2, 7, 2 * PAD, PAIR), BF),
+            pltpu.VMEM((2, 7, 2 * PAD, PAIR), BF),
+            pltpu.VMEM((2, 2, 2, PAD, WIDTH), BF),
             pltpu.VMEM((EXPERTS, PAD, WIDTH), BF),
             pltpu.SemaphoreType.DMA((SENDS,)),
             pltpu.SemaphoreType.DMA((RECVS,)),

time: 130 us -> 119 us (0.915)
  Pallas kernels: 127 us -> 116 us
    pallas_call x1, Pallas kernels: 127 us -> 116 us  [body(): pl.pallas_call(kernel, out_shape=jax.ShapeDtypeStruct(tokens.shape, BF),...]
where the time goes in v3:
time: 119 us; the launch traced here: 117 us
  Pallas kernels  116 us (97%)
  local copies, waits for them, and re-layouts  1.42 us (1%)
    pallas_call x1, Pallas kernels, body(): pl.pallas_call(kernel, out_shape=jax.ShapeDtypeStruct(tokens.shape, BF),...  116 us

profile of v3, /device:TPU:7, one launch (start us, length us, event | category | flops | bytes accessed | tf_op | source)
XLA Modules:
  0.0 117.4 jit_solution(8194600706801603508)
XLA Ops:
  0.0 116.0 %shard_map.64 = bf16[96,192]{1,0:T(8,128)(2,1)} custom-call(bf16[96,192]{1,0:T(8,128)(2,1)} %tokens_ref.1, bf16[96,192]{1,0:T(8,128)(2,1)} %grads_ref.1, f32[2,96]{1,0:T(2,128)} %bitcast.2, s32[2,96]{1,0:T(2,128)} %bitcast.3, bf16[1,2,768,512]{3,2,1,0:T(8,128)(2,1)} %wgu_hbm.1, bf16[1,512,768]{2,1,0:T(8,128)(2,1)} %wd_hbm.1), custom_call_target="tpu_custom_call" | custom-call | tf_op jit(solution)/shard_map/pallas_call | solution.py:403
  116.0 1.4 %copy.8 = bf16[96,192]{1,0:T(8,128)(2,1)} copy(bf16[96,192]{1,0:T(8,128)(2,1)} %shard_map.64) | data formatting | bytes 73728

commit v4 on v3

--- a/solution.py
+++ b/solution.py
@@ -16,7 +16,7 @@
 SLICE = 768
 UNITS = 512
 NEAR_RIGHT = 1
-NEAR_LEFT = 2
+NEAR_LEFT = 1
 ORDER = (4, 5, 3, 2, 6, 1, 7, 0)
 BF = jnp.bfloat16
 F32 = jnp.float32
@@ -74,10 +74,10 @@
 
 
 def kernel(
-    tokens_ref, grads_ref, gates_ref, ids_ref, wgu_hbm, wd_hbm,
+    tokens_hbm, grads_hbm, gates_hbm, ids_hbm, wgu_hbm, wd_hbm,
     result_ref,
     outgoing, arrived, packed, block, xg, wgu, wd, part, part_out, part_in, gu, products, swapped,
-    rows_out, rows_in, back_out, back, send_sem, recv_sem, local_sem,
+    rows_out, rows_in, back_out, back, tokens_ref, grads_ref, gates_ref, ids_ref, send_sem, recv_sem, local_sem,
 ):
     e = lax.axis_index("expert")
     t = lax.axis_index("tensor")
@@ -119,12 +119,22 @@
             )
             signals += 1
 
+    loads = [
+        pltpu.make_async_copy(source, target, local_sem.at[4 + i])
+        for i, (source, target) in enumerate(
+            ((ids_hbm, ids_ref), (tokens_hbm, tokens_ref), (grads_hbm, grads_ref), (gates_hbm, gates_ref))
+        )
+    ]
+    for load in loads:
+        load.start()
     mine = pl.multiple_of(odd * SLICE, SLICE)
     own_gu = pltpu.make_async_copy(wgu_hbm.at[0], wgu.at[:, pl.ds(mine, SLICE), :], local_sem.at[0])
     own_d = pltpu.make_async_copy(wd_hbm.at[0], wd.at[:, pl.ds(mine, SLICE)], local_sem.at[1])
     own_gu.start()
     own_d.start()
 
+    for load in loads:
+        load.wait()
     ids = ids_ref[...]
     count = ids.shape[1]
     lines = iota((EXPERTS, count), 0)
@@ -176,9 +186,11 @@
         source = origin + (1 - same) * (6 + 2 * lax.rem(origin, 2) - 2 * origin)
         return r, source - 4 * h
 
-    def spot(n, kind, origin):
+    def spot(n, kind, origin, first=0, count=ROWS):
         r, pair = holds(origin)
-        return xg.at[n, kind, r, :, pl.ds(pl.multiple_of(pair * PAIR, PAIR), PAIR)]
+        return xg.at[n, kind, r, pl.ds(first, count), pl.ds(pl.multiple_of(pair * PAIR, PAIR), PAIR)]
+
+    opposite = ((0, 96), (96, ROWS - 96))
 
     def repack(n):
         for side in range(2):
@@ -194,7 +206,7 @@
         return here
 
     class Gather:
-        reach = {(0, 0): 4, (1, 0): 3, (0, 1): NEAR_RIGHT, (1, 1): NEAR_LEFT}
+        reach = {(0, 0): 4, (1, 0): 4, (0, 1): NEAR_RIGHT, (1, 1): NEAR_LEFT}
 
         def __init__(self, n):
             self.n = n
@@ -211,7 +223,8 @@
 
         def push(self, way, kind, step, source=None):
             side = z if kind == 0 else 1 - z
-            ref = spot(self.n, side, self.origin(way, step - 1))
+            part = opposite[way] if step == 4 else (0, ROWS)
+            ref = spot(self.n, side, self.origin(way, step - 1), *part)
             self.moves[way, kind, step] = copies.go(ref if source is None else source, ref, right if way == 0 else left)
 
         def swapped(self):
@@ -226,7 +239,8 @@
                     if step < self.reach[way, 0]:
                         self.push(way, 0, step + 1)
                     if step > self.reach[way, 1]:
-                        ref = spot(self.n, z, self.origin(way, step))
+                        part = opposite[way] if step == 4 else (0, ROWS)
+                        ref = spot(self.n, z, self.origin(way, step), *part)
                         self.far.append(copies.go(ref, ref, across))
 
         def other(self, step):
@@ -294,12 +308,10 @@
             rows_out[n, index] = value.astype(BF)
             moves[index] = copies.go(rows_out.at[n, index], rows_in.at[n, index], way)
 
-        for index in (0, 4, 1, 5):
+        for index in (0, 4, 1, 5, 2, 6, 3, 7):
             product(index)
         link(0, right, True)
         link(4, left, True)
-        for index in (2, 6, 3, 7):
-            product(index)
         yield
         link(1, right, False)
         link(5, left, False)
@@ -403,7 +415,7 @@
     return pl.pallas_call(
         kernel,
         out_shape=jax.ShapeDtypeStruct(tokens.shape, BF),
-        in_specs=[vmem, vmem, vmem, vmem, hbm, hbm],
+        in_specs=[hbm] * 6,
         out_specs=vmem,
         scratch_shapes=[
             pltpu.VMEM((2, EXPERTS, PAD, WIDTH), BF),
@@ -423,9 +435,13 @@
             pltpu.VMEM((2, 7, 2 * PAD, PAIR), BF),
             pltpu.VMEM((2, 2, 2, PAD, WIDTH), BF),
             pltpu.VMEM((EXPERTS, PAD, WIDTH), BF),
+            pltpu.VMEM(tokens.shape, BF),
+            pltpu.VMEM(tokens.shape, BF),
+            pltpu.VMEM(gates.shape[::-1], F32),
+            pltpu.VMEM(gates.shape[::-1], jnp.int32),
             pltpu.SemaphoreType.DMA((SENDS,)),
             pltpu.SemaphoreType.DMA((RECVS,)),
-            pltpu.SemaphoreType.DMA((4,)),
+            pltpu.SemaphoreType.DMA((8,)),
         ],
         compiler_params=pltpu.CompilerParams(
             collective_id=0, has_side_effects=True, vmem_limit_bytes=56 * 1024 * 1024

time: 119 us -> 118 us (level)
  no operation moved by 1% of the time
where the time goes in v4:
time: 118 us; the launch traced here: 117 us
  Pallas kernels  116 us (98%)
  local copies, waits for them, and re-layouts  1.42 us (1%)
    pallas_call x1, Pallas kernels, body(): pl.pallas_call(kernel, out_shape=jax.ShapeDtypeStruct(tokens.shape, BF),...  116 us

profile of v4, /device:TPU:7, one launch (start us, length us, event | category | flops | bytes accessed | tf_op | source)
XLA Modules:
  0.0 117.0 jit_solution(8911846286287863881)
XLA Ops:
  0.0 115.6 %shard_map.64 = bf16[96,192]{1,0:T(8,128)(2,1)} custom-call(bf16[96,192]{1,0:T(8,128)(2,1)} %tokens_hbm.1, bf16[96,192]{1,0:T(8,128)(2,1)} %grads_hbm.1, f32[2,96]{1,0:T(2,128)} %bitcast.2, s32[2,96]{1,0:T(2,128)} %bitcast.3, bf16[1,2,768,512]{3,2,1,0:T(8,128)(2,1)} %wgu_hbm.1, bf16[1,512,768]{2,1,0:T(8,128)(2,1)} %wd_hbm.1), custom_call_target="tpu_custom_call" | custom-call | tf_op jit(solution)/shard_map/pallas_call | solution.py:415
  115.6 1.4 %copy.8 = bf16[96,192]{1,0:T(8,128)(2,1)} copy(bf16[96,192]{1,0:T(8,128)(2,1)} %shard_map.64) | data formatting | bytes 73728

commit v5 on v4

--- a/solution.py
+++ b/solution.py
@@ -109,15 +109,16 @@
 
     barrier = pltpu.get_barrier_semaphore()
     signals = 0
-    for peer in (right, left, across, weights_peer, rows_peer, mirror):
-        pl.semaphore_signal(barrier, inc=1, device_id=peer, device_id_type=MESH)
-        signals += 1
-    for other in range(EXPERTS):
+    for turn in ORDER:
+        other = lax.rem(e + turn, EXPERTS)
         for side in range(2):
             pl.semaphore_signal(
                 barrier, inc=1, device_id={"expert": other, "tensor": 2 * y + side}, device_id_type=MESH
             )
             signals += 1
+    for peer in (right, left, across, weights_peer, rows_peer, mirror):
+        pl.semaphore_signal(barrier, inc=1, device_id=peer, device_id_type=MESH)
+        signals += 1
 
     loads = [
         pltpu.make_async_copy(source, target, local_sem.at[4 + i])

time: 118 us -> 118 us (level)
  no operation moved by 1% of the time
where the time goes in v5:
time: 118 us; the launch traced here: 116 us
  Pallas kernels  115 us (97%)
  local copies, waits for them, and re-layouts  1.42 us (1%)
    pallas_call x1, Pallas kernels, body(): pl.pallas_call(kernel, out_shape=jax.ShapeDtypeStruct(tokens.shape, BF),...  115 us

profile of v5, /device:TPU:7, one launch (start us, length us, event | category | flops | bytes accessed | tf_op | source)
XLA Modules:
  0.0 116.3 jit_solution(18247332994717264659)
XLA Ops:
  0.0 114.9 %shard_map.64 = bf16[96,192]{1,0:T(8,128)(2,1)} custom-call(bf16[96,192]{1,0:T(8,128)(2,1)} %tokens_hbm.1, bf16[96,192]{1,0:T(8,128)(2,1)} %grads_hbm.1, f32[2,96]{1,0:T(2,128)} %bitcast.2, s32[2,96]{1,0:T(2,128)} %bitcast.3, bf16[1,2,768,512]{3,2,1,0:T(8,128)(2,1)} %wgu_hbm.1, bf16[1,512,768]{2,1,0:T(8,128)(2,1)} %wd_hbm.1), custom_call_target="tpu_custom_call" | custom-call | tf_op jit(solution)/shard_map/pallas_call | solution.py:416
  114.9 1.4 %copy.8 = bf16[96,192]{1,0:T(8,128)(2,1)} copy(bf16[96,192]{1,0:T(8,128)(2,1)} %shard_map.64) | data formatting | bytes 73728
